TPU v7x, 768 devices: a whole 4x8x12 slice. The times are simulated.
768 devices in a mesh: batch: 8 (over y), dir: 96 (over z, x, core).
Axes of the slice: x: 4, y: 8, z: 12, core: 2. Of those that a mesh axis runs over, the one named last changes fastest.
Arguments:
- embeddings: bfloat16 [3072, 2048], P(('batch', 'dir')), may hold values from -13 to 13
- directions: bfloat16 [2048, 24576], P(None, 'dir'), may hold values from -0.125 to 0.125
Outputs:
- grad_embed: float32 [3072, 2048], P(('batch', 'dir'))
All inputs are finite; a program needn't handle non-finite values.
Results may differ from a plain program's by a relative error of at most 0.0016.
Values may be sent and summed in bfloat16 or wider, within the bound.
No kernel may reach another device: no remote copies, remote signals or barrier semaphores. Data moves between devices by JAX's collectives and lax.ppermute only.
A program may use at most 32 MiB of HBM per device.

v0:
```python
import functools
import math

import jax
import jax.numpy as jnp
from jax import lax
from jax.experimental import pallas as pl
from jax.experimental.pallas import tpu as pltpu
from jax.sharding import Mesh, PartitionSpec as P


KNOTS = 17
STEP = 3.0 / (KNOTS - 1)
KNOT = [k * STEP for k in range(KNOTS)]
TARGET = [math.exp(-0.5 * t * t) for t in KNOT]
WEIGHT = [(0.5 if k in (0, KNOTS - 1) else 1.0) * STEP * TARGET[k] for k in range(KNOTS)]
TURN = (6.28125, 0.0019340515136719, 1.2556659146e-06)
TILE = 16
F32 = jnp.float32
BF16 = jnp.bfloat16
LINK = jnp.float16


def base_angle(proj):
    theta = proj * STEP
    turns = jnp.round(theta * (0.5 / math.pi))
    q = 0.25 * (((theta - turns * TURN[0]) - turns * TURN[1]) - turns * TURN[2])
    z = q * q
    s = q * (1.0 + z * (-1.0 / 6 + z * (1.0 / 120 + z * (-1.0 / 5040 + z * (1.0 / 362880)))))
    c = 1.0 - z * (0.5 + z * (-1.0 / 24 + z * (1.0 / 720 + z * (-1.0 / 40320))))
    s2 = 2.0 * s * c
    c2 = 1.0 - 2.0 * s * s
    return 1.0 - 2.0 * s2 * s2, 2.0 * s2 * c2


def unit_kernel(dir_ref, unit_ref):
    width = dir_ref.shape[1]
    rows = 256
    total = jnp.zeros((8, width), F32)
    for i in range(dir_ref.shape[0] // rows):
        w = dir_ref[pl.ds(i * rows, rows), :].astype(F32)
        total = total + jnp.sum((w * w).reshape(rows // 8, 8, width), axis=0)
    inv = 1.0 / jnp.sqrt(jnp.sum(total, axis=0, keepdims=True) + 1e-06)
    for i in range(dir_ref.shape[0] // rows):
        w = dir_ref[pl.ds(i * rows, rows), :].astype(F32)
        unit_ref[pl.ds(i * rows, rows), :] = (w * inv).astype(BF16)


def sums_kernel(rows_ref, unit_ref, c_ref, s_ref, out_ref, proj_ref, acc_ref):
    rows, width = proj_ref.shape
    tile = 2 * TILE
    proj_ref[...] = jnp.dot(rows_ref[...], unit_ref[...], preferred_element_type=F32)
    acc_ref[...] = jnp.zeros_like(acc_ref)

    def fold(v):
        return jnp.sum(v.reshape(tile // 8, 8, width), axis=0)

    @pl.loop(0, rows // tile)
    def _(i):
        at = pl.ds(pl.multiple_of(i * tile, tile), tile)
        c1, s1 = base_angle(proj_ref[at, :])
        c_ref[at, :] = c1
        s_ref[at, :] = s1
        two = c1 + c1
        acc_ref[0] += fold(c1)
        acc_ref[KNOTS - 1] += fold(s1)
        cp, sp, cc, sc = jnp.ones_like(c1), jnp.zeros_like(c1), c1, s1
        for k in range(1, KNOTS - 1):
            cp, cc = cc, two * cc - cp
            sp, sc = sc, two * sc - sp
            acc_ref[k] += fold(cc)
            acc_ref[KNOTS - 1 + k] += fold(sc)

    out_ref[...] = jnp.sum(acc_ref[...], axis=1)
    for k in range(1, KNOTS):
        out_ref[pl.ds(k - 1, 1), :] -= rows * TARGET[k]


def grad_kernel(total_rows, steps, along_x, c_ref, s_ref, c2_ref, s2_ref, sums_ref, sums2_ref, unit_ref, more_ref, *refs):
    out_refs, (g_ref, rep_ref) = refs[:-2], refs[-2:]
    rows, width = g_ref.shape
    block = rows // len(steps)
    here = lax.axis_index("x")
    sums = jnp.concatenate([sums_ref[...], sums2_ref[...]], axis=1)
    for k in range(KNOTS):
        if k == 0:
            cos_off = jnp.full((1, width), total_rows * (1.0 - TARGET[0]), F32)
            sin_total = jnp.zeros((1, width), F32)
        else:
            cos_off = sums[k - 1 : k]
            sin_total = sums[KNOTS + k - 2 : KNOTS + k - 1]
        cos_coef = 2.0 * WEIGHT[k] * (cos_off / total_rows)
        sin_coef = 2.0 * WEIGHT[k] * (sin_total / total_rows)
        rep_ref[k] = jnp.broadcast_to(KNOT[k] * sin_coef, (8, width))
        rep_ref[KNOTS + k] = jnp.broadcast_to(-KNOT[k] * cos_coef, (8, width))

    def tile(i, chip):
        at = pl.ds(pl.multiple_of((i * along_x + chip) * TILE, TILE), TILE)
        c1 = jnp.concatenate([c_ref[at, :], c2_ref[at, :]], axis=1).reshape(TILE // 8, 8, width)
        s1 = jnp.concatenate([s_ref[at, :], s2_ref[at, :]], axis=1).reshape(TILE // 8, 8, width)
        two = c1 + c1
        a2 = jnp.zeros_like(c1)
        b2 = a2
        a1 = rep_ref[KNOTS - 1] + a2
        b1 = rep_ref[2 * KNOTS - 1] + a2
        for k in range(KNOTS - 2, 0, -1):
            a1, a2 = rep_ref[k] + (two * a1 - a2), a1
            b1, b2 = rep_ref[KNOTS + k] + (two * b1 - b2), b1
        g = rep_ref[0] + (c1 * a1 - a2) + s1 * b1
        return g.reshape(TILE, width).astype(BF16)

    for j, by in enumerate(steps):

        @pl.loop(0, block // TILE)
        def _(i):
            at = pl.ds(pl.multiple_of(j * block + i * TILE, TILE), TILE)
            g_ref[at, :] = tile(i, lax.rem(here + by, along_x))

    step, half = 512, width // 2
    for i in range(unit_ref.shape[0] // step):
        at = pl.ds(i * step, step)
        out = times_transposed(g_ref[:, pl.ds(0, half)], unit_ref[at, :]) + times_transposed(
            g_ref[:, pl.ds(half, half)], more_ref[at, :]
        )
        for j, out_ref in enumerate(out_refs):
            out_ref[:, at] = out[j * block : (j + 1) * block]


def times_transposed(a, b):
    return lax.dot_general(a, b, (((1,), (1,)), ((), ())), preferred_element_type=F32)


def call(kernel, outs, scratch, flops, moved, operands):
    whole = pl.BlockSpec(memory_space=pltpu.VMEM)
    return pl.pallas_call(
        kernel,
        out_shape=outs,
        in_specs=[whole] * operands,
        out_specs=jax.tree.map(lambda _: whole, outs),
        scratch_shapes=scratch,
        compiler_params=pltpu.CompilerParams(vmem_limit_bytes=16 << 20),
        cost_estimate=pl.CostEstimate(flops=flops, bytes_accessed=moved, transcendentals=0),
    )


def to_all(x, axes, peers):
    return lax.all_to_all(jnp.broadcast_to(x[None], (peers,) + x.shape), axes, 0, 0, tiled=True)


def turn(x, axis, by):
    n = lax.axis_size(axis)
    return lax.ppermute(x, axis, [(i, (i + by) % n) for i in range(n)])


def local(embeddings, directions):
    zh, zl, along_x = lax.axis_size("zh"), lax.axis_size("zl"), lax.axis_size("x")
    batch = lax.axis_size("y")
    depth, width = directions.shape
    block = embeddings.shape[0] * zh * zl
    rows = block * along_x
    total_rows = float(2 * rows * batch)
    sds = jax.ShapeDtypeStruct

    held = to_all(embeddings, "zh", zh).reshape(-1, depth)
    theirs = turn(directions, "c", 1)
    units = []
    for columns in (directions, theirs):
        units.append(call(unit_kernel, sds((depth, width), BF16), (), 4 * depth * width, 4 * depth * width, 1)(columns))
    held, units = lax.optimization_barrier((held, units))
    held = to_all(held, ("zl", "x"), zl * along_x).reshape(rows, depth)

    def sums_of(unit):
        return call(
            sums_kernel,
            (sds((rows, width), F32), sds((rows, width), F32), sds((2 * KNOTS - 2, width), F32)),
            (pltpu.VMEM((rows, width), F32), pltpu.VMEM((2 * KNOTS - 2, 8, width), F32)),
            2 * rows * depth * width,
            4 * rows * depth,
            2,
        )(held, unit)

    c2, s2, sums = sums_of(units[1])
    arrived = turn(sums, "c", 1)
    c1, s1, sums = sums_of(units[0])
    sums = to_all((sums + arrived).astype(LINK), "y", batch)
    sums = jnp.sum(sums.astype(F32), axis=0)
    sums2 = turn(sums, "c", 1)

    def grad(steps):
        outs = call(
            functools.partial(grad_kernel, total_rows, steps, along_x),
            [sds((block, depth), F32)] * len(steps),
            (pltpu.VMEM((len(steps) * block, 2 * width), BF16), pltpu.VMEM((2 * KNOTS, 8, 2 * width), F32)),
            4 * len(steps) * block * depth * width,
            4 * len(steps) * block * depth,
            8,
        )(c1, s1, c2, s2, sums, sums2, *units)
        return dict(zip(steps, outs))

    parts = grad((2, 1, along_x - 1, 0))
    for by in (2, 1, along_x - 1):
        parts[by] = turn(parts[by].astype(LINK), "x", by)
    part = sum(p.astype(F32) for p in parts.values()).astype(LINK)
    part = lax.all_to_all(part.reshape(zl * zh, -1, depth), ("zl", "zh"), 0, 0, tiled=True)
    return jnp.sum(part.astype(F32), axis=0)


def solution(mesh):
    fine = Mesh(mesh.devices.reshape(8, 4, 3, 4, 2), ("y", "zh", "zl", "x", "c"))
    along = ("zh", "zl", "x", "c")
    rows = P(("y",) + along, None)

    return jax.shard_map(local, mesh=fine, in_specs=(rows, P(None, along)), out_specs=rows, check_vma=False)
```

profile of v0, /device:TPU:6, one launch (start us, length us, event | category | flops | bytes accessed | tf_op | source)
XLA Modules:
  0.0 110.2 jit_solution(11808170800235414634)
XLA Ops:
  0.0 1.9 %collective-permute-start = (bf16[2048,256]{1,0:T(8,128)(2,1)}, bf16[2048,256]{1,0:T(8,128)(2,1)S(1)}, u32[]{:S(2)}, u32[]{:S(2)}) collective-permute-start(bf16[2048,256]{1,0:T(8,128)(2,1)} %dir_ref.1), channel_id=1, source_target_pairs={{0,1},{1,0},{2,3},{3,2},{4,5},{5,4},{6,7},{7,6},{8,9},{9,8},{10,11... | collective-permute-start | bytes 3145736 | tf_op jit(solution)/shard_map/ppermute | solution.py:152
  1.9 1.4 %broadcast_in_dim.6 = bf16[4,4,2048]{2,1,0:T(4,128)(2,1)} broadcast(bf16[4,2048]{1,0:T(4,128)(2,1)} %param.2), dimensions={1,2} | broadcast | bytes 81920 | tf_op jit(solution)/shard_map/broadcast_in_dim | solution.py:147
  3.3 14.5 %all-to-all-start = ((bf16[4,4,2048]{2,1,0:T(4,128)(2,1)}), bf16[4,4,2048]{2,1,0:T(4,128)(2,1)S(1)}, u32[]{:S(2)}, u32[]{:S(2)}) async-start(bf16[4,4,2048]{2,1,0:T(4,128)(2,1)} %broadcast_in_dim.6), calls=%async_computation | async-start | bytes 131072 | tf_op jit(solution)/shard_map/all_to_all | solution.py:147
  17.8 0.0 copy-start
  17.8 1.2 %copy-done = bf16[2048,256]{1,0:T(8,128)(2,1)S(1)} copy-done((bf16[2048,256]{1,0:T(8,128)(2,1)S(1)}, bf16[2048,256]{1,0:T(8,128)(2,1)}, u32[]{:S(2)}) %copy-start) | copy-done | bytes 1048600
  19.0 0.3 shard_map.28.unit_ref
  19.3 9.8 %all-to-all-done = bf16[4,4,2048]{2,1,0:T(4,128)(2,1)S(1)} async-done(((bf16[4,4,2048]{2,1,0:T(4,128)(2,1)}), bf16[4,4,2048]{2,1,0:T(4,128)(2,1)S(1)}, u32[]{:S(2)}, u32[]{:S(2)}) %all-to-all-start) | async-done | bytes 65568 | tf_op jit(solution)/shard_map/all_to_all | solution.py:147
  29.1 0.0 collective-permute-done.dir_ref
  29.1 0.3 shard_map.29.unit_ref.more_ref
  29.3 0.1 broadcast_in_dim.7
  29.4 19.1 %all_to_all.20 = bf16[12,16,2048]{2,1,0:T(8,128)(2,1)S(1)} all-to-all(bf16[12,16,2048]{2,1,0:T(8,128)(2,1)S(1)} %broadcast_in_dim.7), channel_id=1, replica_groups=mesh['y'=8,'zh'=4,'zl'=3,'x'=4,'c'=2] {'zl','x'}, dimensions={0} | all-to-all | bytes 1572864 | tf_op jit(solution)/shard_map/all_to_all | solution.py:147
  48.6 1.3 %shard_map.31 = (f32[192,256]{1,0:T(8,128)S(1)}, f32[192,256]{1,0:T(8,128)S(1)}, f32[32,256]{1,0:T(8,128)S(1)}) custom-call(bf16[192,2048]{1,0:T(8,128)(2,1)S(1)} %bitcast.1, bf16[2048,256]{1,0:T(8,128)(2,1)S(1)} %shard_map.29.unit_ref.more_ref), custom_call_target="tpu_custom_call" | custom-call | flops 201326592 | bytes 1572864 | tf_op jit(solution)/shard_map/pallas_call | solution.py:173
  49.9 1.9 %collective-permute-start.1 = (f32[32,256]{1,0:T(8,128)S(1)}, f32[32,256]{1,0:T(8,128)S(1)}, u32[]{:S(2)}, u32[]{:S(2)}) collective-permute-start(f32[32,256]{1,0:T(8,128)S(1)} %get-tuple-element.26), channel_id=1, source_target_pairs={{0,1},{1,0},{2,3},{3,2},{4,5},{5,4},{6,7},{7,6},{8,9},{9,8},{10,11... | collective-permute-start | bytes 98312 | tf_op jit(solution)/shard_map/ppermute | solution.py:152
  51.8 1.3 %shard_map.30 = (f32[192,256]{1,0:T(8,128)S(1)}, f32[192,256]{1,0:T(8,128)S(1)}, f32[32,256]{1,0:T(8,128)S(1)}) custom-call(bf16[192,2048]{1,0:T(8,128)(2,1)S(1)} %bitcast.2, bf16[2048,256]{1,0:T(8,128)(2,1)S(1)} %shard_map.28.unit_ref), custom_call_target="tpu_custom_call" | custom-call | flops 201326592 | bytes 1572864 | tf_op jit(solution)/shard_map/pallas_call | solution.py:173
  53.1 0.0 collective-permute-done.1
  53.2 16.6 %all_to_all.21 = f16[8,32,256]{2,1,0:T(8,128)(2,1)S(1)} all-to-all(f16[8,32,256]{2,1,0:T(8,128)(2,1)S(1)} %broadcast_in_dim.8), channel_id=1, replica_groups=mesh['y'=8,'zh'=4,'zl'=3,'x'=4,'c'=2] {'y'}, dimensions={0} | all-to-all | bytes 262144 | tf_op jit(solution)/shard_map/all_to_all | solution.py:147
  69.8 1.9 %collective-permute-start.2 = (f32[32,256]{1,0:T(8,128)S(1)}, f32[32,256]{1,0:T(8,128)S(1)}, u32[]{:S(2)}, u32[]{:S(2)}) collective-permute-start(f32[32,256]{1,0:T(8,128)S(1)} %convert_reduce_fusion.1.sums_ref), channel_id=1, source_target_pairs={{0,1},{1,0},{2,3},{3,2},{4,5},{5,4},{6,7},{7,6},{8,9},{9,8},{10,11... | collective-permute-start | bytes 98312 | tf_op jit(solution)/shard_map/ppermute | solution.py:152
  71.8 1.2 %collective-permute-done.2.sums2_ref = f32[32,256]{1,0:T(8,128)S(1)} collective-permute-done((f32[32,256]{1,0:T(8,128)S(1)}, f32[32,256]{1,0:T(8,128)S(1)}, u32[]{:S(2)}, u32[]{:S(2)}) %collective-permute-start.2) | collective-permute-done | bytes 32800 | tf_op jit(solution)/shard_map/ppermute | solution.py:152
  72.9 2.3 %shard_map.32 = (f32[48,2048]{1,0:T(8,128)S(1)}, f32[48,2048]{1,0:T(8,128)S(1)}, f32[48,2048]{1,0:T(8,128)S(1)}, f32[48,2048]{1,0:T(8,128)S(1)}) custom-call(f32[192,256]{1,0:T(8,128)S(1)} %get-tuple-element.20.c_ref, f32[192,256]{1,0:T(8,128)S(1)} %get-tuple-element.21.s_ref, f32[192,256]{1,0:T(8,128)S(1)} %get-tuple-element.23.c2_ref, ...), custom_call_target="tpu_custom_call" | custom-call | flops 402653184 | bytes 1572864 | tf_op jit(solution)/shard_map/pallas_call | solution.py:190
  75.3 1.9 %collective-permute-start.5 = (f16[48,2048]{1,0:T(8,128)(2,1)S(1)}, f16[48,2048]{1,0:T(8,128)(2,1)S(1)}, u32[]{:S(2)}, u32[]{:S(2)}) collective-permute-start(f16[48,2048]{1,0:T(8,128)(2,1)S(1)} %convert_element_type.36), channel_id=1, source_target_pairs={{0,6},{2,0},{4,2},{6,4},{1,7},{3,1},{5,3},{7,5},{8,14},{10,8},{12,... | collective-permute-start | bytes 589832 | tf_op jit(solution)/shard_map/ppermute | solution.py:152
  77.2 5.1 %collective-permute-start.4 = (f16[48,2048]{1,0:T(8,128)(2,1)S(1)}, f16[48,2048]{1,0:T(8,128)(2,1)S(1)}, u32[]{:S(2)}, u32[]{:S(2)}) collective-permute-start(f16[48,2048]{1,0:T(8,128)(2,1)S(1)} %convert_element_type.34), channel_id=1, source_target_pairs={{0,2},{2,4},{4,6},{6,0},{1,3},{3,5},{5,7},{7,1},{8,10},{10,12},{12... | collective-permute-start | bytes 589832 | tf_op jit(solution)/shard_map/ppermute | solution.py:152
  82.4 1.9 %collective-permute-start.3 = (f16[48,2048]{1,0:T(8,128)(2,1)S(1)}, f16[48,2048]{1,0:T(8,128)(2,1)S(1)}, u32[]{:S(2)}, u32[]{:S(2)}) collective-permute-start(f16[48,2048]{1,0:T(8,128)(2,1)S(1)} %convert_element_type.32), channel_id=1, source_target_pairs={{0,4},{2,6},{4,0},{6,2},{1,5},{3,7},{5,1},{7,3},{8,12},{10,14},{12... | collective-permute-start | bytes 589832 | tf_op jit(solution)/shard_map/ppermute | solution.py:152
  84.3 1.1 collective-permute-done.5
  85.4 5.4 %collective-permute-done.4 = f16[48,2048]{1,0:T(8,128)(2,1)S(1)} collective-permute-done((f16[48,2048]{1,0:T(8,128)(2,1)S(1)}, f16[48,2048]{1,0:T(8,128)(2,1)S(1)}, u32[]{:S(2)}, u32[]{:S(2)}) %collective-permute-start.4) | collective-permute-done | bytes 196640 | tf_op jit(solution)/shard_map/ppermute | solution.py:152
  90.7 1.4 %collective-permute-done.3 = f16[48,2048]{1,0:T(8,128)(2,1)S(1)} collective-permute-done((f16[48,2048]{1,0:T(8,128)(2,1)S(1)}, f16[48,2048]{1,0:T(8,128)(2,1)S(1)}, u32[]{:S(2)}, u32[]{:S(2)}) %collective-permute-start.3) | collective-permute-done | bytes 196640 | tf_op jit(solution)/shard_map/ppermute | solution.py:152
  92.2 0.1 add_convert_fusion
  92.3 0.1 reshape.14
  92.4 17.1 %all_to_all.22 = f16[12,4,2048]{2,1,0:T(4,128)(2,1)S(1)} all-to-all(f16[12,4,2048]{2,1,0:T(4,128)(2,1)S(1)} %reshape.14), channel_id=1, replica_groups=mesh['y'=8,'zh'=4,'zl'=3,'x'=4,'c'=2] {'zl','zh'}, dimensions={0} | all-to-all | bytes 393216 | tf_op jit(solution)/shard_map/all_to_all | solution.py:204
  109.4 0.7 convert_reduce_fusion
  (7 shorter events, 0.1 us)
Async XLA Ops:
  0.0 29.1 %collective-permute-start = (bf16[2048,256]{1,0:T(8,128)(2,1)}, bf16[2048,256]{1,0:T(8,128)(2,1)S(1)}, u32[]{:S(2)}, u32[]{:S(2)}) collective-permute-start(bf16[2048,256]{1,0:T(8,128)(2,1)} %dir_ref.1), channel_id=1, source_target_pairs={{0,1},{1,0},{2,3},{3,2},{4,5},{5,4},{6,7},{7,6},{8,9},{9,8},{10,11... | collective-permute-start | bytes 3145736 | tf_op jit(solution)/shard_map/ppermute | solution.py:152
  3.3 25.8 %all-to-all-start = ((bf16[4,4,2048]{2,1,0:T(4,128)(2,1)}), bf16[4,4,2048]{2,1,0:T(4,128)(2,1)S(1)}, u32[]{:S(2)}, u32[]{:S(2)}) async-start(bf16[4,4,2048]{2,1,0:T(4,128)(2,1)} %broadcast_in_dim.6), calls=%async_computation | async-start | bytes 131072 | tf_op jit(solution)/shard_map/all_to_all | solution.py:147
  17.8 1.2 %copy-start = (bf16[2048,256]{1,0:T(8,128)(2,1)S(1)}, bf16[2048,256]{1,0:T(8,128)(2,1)}, u32[]{:S(2)}) copy-start(bf16[2048,256]{1,0:T(8,128)(2,1)} %dir_ref.1) | copy-start | bytes 3145732
  49.9 3.2 %collective-permute-start.1 = (f32[32,256]{1,0:T(8,128)S(1)}, f32[32,256]{1,0:T(8,128)S(1)}, u32[]{:S(2)}, u32[]{:S(2)}) collective-permute-start(f32[32,256]{1,0:T(8,128)S(1)} %get-tuple-element.26), channel_id=1, source_target_pairs={{0,1},{1,0},{2,3},{3,2},{4,5},{5,4},{6,7},{7,6},{8,9},{9,8},{10,11... | collective-permute-start | bytes 98312 | tf_op jit(solution)/shard_map/ppermute | solution.py:152
  69.8 3.1 %collective-permute-start.2 = (f32[32,256]{1,0:T(8,128)S(1)}, f32[32,256]{1,0:T(8,128)S(1)}, u32[]{:S(2)}, u32[]{:S(2)}) collective-permute-start(f32[32,256]{1,0:T(8,128)S(1)} %convert_reduce_fusion.1.sums_ref), channel_id=1, source_target_pairs={{0,1},{1,0},{2,3},{3,2},{4,5},{5,4},{6,7},{7,6},{8,9},{9,8},{10,11... | collective-permute-start | bytes 98312 | tf_op jit(solution)/shard_map/ppermute | solution.py:152
  75.3 10.1 %collective-permute-start.5 = (f16[48,2048]{1,0:T(8,128)(2,1)S(1)}, f16[48,2048]{1,0:T(8,128)(2,1)S(1)}, u32[]{:S(2)}, u32[]{:S(2)}) collective-permute-start(f16[48,2048]{1,0:T(8,128)(2,1)S(1)} %convert_element_type.36), channel_id=1, source_target_pairs={{0,6},{2,0},{4,2},{6,4},{1,7},{3,1},{5,3},{7,5},{8,14},{10,8},{12,... | collective-permute-start | bytes 589832 | tf_op jit(solution)/shard_map/ppermute | solution.py:152
  77.2 13.5 %collective-permute-start.4 = (f16[48,2048]{1,0:T(8,128)(2,1)S(1)}, f16[48,2048]{1,0:T(8,128)(2,1)S(1)}, u32[]{:S(2)}, u32[]{:S(2)}) collective-permute-start(f16[48,2048]{1,0:T(8,128)(2,1)S(1)} %convert_element_type.34), channel_id=1, source_target_pairs={{0,2},{2,4},{4,6},{6,0},{1,3},{3,5},{5,7},{7,1},{8,10},{10,12},{12... | collective-permute-start | bytes 589832 | tf_op jit(solution)/shard_map/ppermute | solution.py:152
  82.4 9.8 %collective-permute-start.3 = (f16[48,2048]{1,0:T(8,128)(2,1)S(1)}, f16[48,2048]{1,0:T(8,128)(2,1)S(1)}, u32[]{:S(2)}, u32[]{:S(2)}) collective-permute-start(f16[48,2048]{1,0:T(8,128)(2,1)S(1)} %convert_element_type.32), channel_id=1, source_target_pairs={{0,4},{2,6},{4,0},{6,2},{1,5},{3,7},{5,1},{7,3},{8,12},{10,14},{12... | collective-permute-start | bytes 589832 | tf_op jit(solution)/shard_map/ppermute | solution.py:152
where the time goes:
time: 112 us; the launch traced here: 110 us
  blocking collectives  52.9 us (47%)
  starting transfers between devices  29.2 us (26%)
  waiting for transfers between devices  18.8 us (17%)
  Pallas kernels  5.39 us (5%)
  local copies, waits for them, and re-layouts  2.78 us (2%)
    all_to_all x2, blocking collectives, to_all(): lax.all_to_all(jnp.broadcast_to(x[None], (peers,) + x.shape), axes, 0, 0,...  35.8 us
    all_to_all x1, blocking collectives, local(): lax.all_to_all(part.reshape(zl * zh, -1, depth), ('zl', 'zh'), 0, 0, tile...  17.1 us
    ppermute x6, starting transfers between devices, turn(): return lax.ppermute(x, axis, [(i, (i + by) % n) for i in range(n)])  14.7 us
    all_to_all x1, starting transfers between devices, to_all(): lax.all_to_all(jnp.broadcast_to(x[None], (peers,) + x.shape), axes, 0, 0,...  14.5 us
    all_to_all x1, waiting for transfers between devices, to_all(): lax.all_to_all(jnp.broadcast_to(x[None], (peers,) + x.shape), axes, 0, 0,...  9.77 us
    ppermute x6, waiting for transfers between devices, turn(): return lax.ppermute(x, axis, [(i, (i + by) % n) for i in range(n)])  9.05 us
    pallas_call x2, Pallas kernels, sums_of(): call(sums_kernel, (sds((rows, width), F32), sds((rows, width), F32), sds(...  2.61 us
    pallas_call x1, Pallas kernels, grad(): call(functools.partial(grad_kernel, total_rows, steps, along_x), [sds((bl...  2.26 us
  transfers between devices with their start and end apart: 7, of which 5 were waited for; matrix products, arithmetic and copies ran while one was open for 1% of the time, Pallas kernels for 1%

commit v1 on v0

--- a/solution.py
+++ b/solution.py
@@ -76,12 +76,14 @@
         out_ref[pl.ds(k - 1, 1), :] -= rows * TARGET[k]
 
 
-def grad_kernel(total_rows, steps, along_x, c_ref, s_ref, c2_ref, s2_ref, sums_ref, sums2_ref, unit_ref, more_ref, *refs):
+def grad_kernel(total_rows, steps, along_x, c_ref, s_ref, c2_ref, s2_ref, sums_ref, unit_ref, more_ref, *refs):
     out_refs, (g_ref, rep_ref) = refs[:-2], refs[-2:]
     rows, width = g_ref.shape
     block = rows // len(steps)
     here = lax.axis_index("x")
-    sums = jnp.concatenate([sums_ref[...], sums2_ref[...]], axis=1)
+    core = lax.axis_index("c")
+    sums = [jnp.sum(sums_ref[:, pl.ds(i, 1)], axis=(0, 1)) for i in (core, 1 - core)]
+    sums = jnp.concatenate(sums, axis=1)
     for k in range(KNOTS):
         if k == 0:
             cos_off = jnp.full((1, width), total_rows * (1.0 - TARGET[0]), F32)
@@ -166,7 +168,6 @@
     units = []
     for columns in (directions, theirs):
         units.append(call(unit_kernel, sds((depth, width), BF16), (), 4 * depth * width, 4 * depth * width, 1)(columns))
-    held, units = lax.optimization_barrier((held, units))
     held = to_all(held, ("zl", "x"), zl * along_x).reshape(rows, depth)
 
     def sums_of(unit):
@@ -182,9 +183,8 @@
     c2, s2, sums = sums_of(units[1])
     arrived = turn(sums, "c", 1)
     c1, s1, sums = sums_of(units[0])
-    sums = to_all((sums + arrived).astype(LINK), "y", batch)
-    sums = jnp.sum(sums.astype(F32), axis=0)
-    sums2 = turn(sums, "c", 1)
+    sums = to_all((sums + arrived).astype(LINK), ("y", "c"), 2 * batch).astype(F32)
+    sums = sums.reshape(batch, 2, 2 * KNOTS - 2, width)
 
     def grad(steps):
         outs = call(
@@ -193,8 +193,8 @@
             (pltpu.VMEM((len(steps) * block, 2 * width), BF16), pltpu.VMEM((2 * KNOTS, 8, 2 * width), F32)),
             4 * len(steps) * block * depth * width,
             4 * len(steps) * block * depth,
-            8,
-        )(c1, s1, c2, s2, sums, sums2, *units)
+            7,
+        )(c1, s1, c2, s2, sums, *units)
         return dict(zip(steps, outs))
 
     parts = grad((2, 1, along_x - 1, 0))

time: 112 us -> 109 us (0.973)
  starting transfers between devices: 29.2 us -> 18.7 us
  blocking collectives: 52.9 us -> 61.1 us
    all_to_all x1, starting transfers between devices: 14.5 us -> 5.85 us  [to_all(): lax.all_to_all(jnp.broadcast_to(x[None], (peers,) + x.shape), axes, 0, 0,...]
    all_to_all x2, blocking collectives: 35.8 us -> 43.3 us  [to_all(): lax.all_to_all(jnp.broadcast_to(x[None], (peers,) + x.shape), axes, 0, 0,...]
    ppermute x6 -> x5, waiting for transfers between devices: 9.05 us -> 11.2 us  [turn(): return lax.ppermute(x, axis, [(i, (i + by) % n) for i in range(n)])]
    ppermute x6 -> x5, starting transfers between devices: 14.7 us -> 12.8 us  [turn(): return lax.ppermute(x, axis, [(i, (i + by) % n) for i in range(n)])]
    all_to_all x1, waiting for transfers between devices: 9.77 us -> 8.41 us  [to_all(): lax.all_to_all(jnp.broadcast_to(x[None], (peers,) + x.shape), axes, 0, 0,...]
    unnamed x2, local copies, waits for them, and re-layouts: 1.22 us -> 0.01 us
  transfers between devices with their start and end apart: 7 -> 6, of which waited for: 5 -> 5; matrix products, arithmetic and copies ran while one was open for 1% -> 0% of each run, Pallas kernels for 1% -> 2%
where the time goes in v1:
time: 109 us; the launch traced here: 108 us
  blocking collectives  61.1 us (56%)
  waiting for transfers between devices  19.6 us (18%)
  starting transfers between devices  18.7 us (17%)
  Pallas kernels  5.42 us (5%)
  local copies, waits for them, and re-layouts  1.84 us (2%)
    all_to_all x2, blocking collectives, to_all(): lax.all_to_all(jnp.broadcast_to(x[None], (peers,) + x.shape), axes, 0, 0,...  43.3 us
    all_to_all x1, blocking collectives, local(): lax.all_to_all(part.reshape(zl * zh, -1, depth), ('zl', 'zh'), 0, 0, tile...  17.8 us
    ppermute x5, starting transfers between devices, turn(): return lax.ppermute(x, axis, [(i, (i + by) % n) for i in range(n)])  12.8 us
    ppermute x5, waiting for transfers between devices, turn(): return lax.ppermute(x, axis, [(i, (i + by) % n) for i in range(n)])  11.2 us
    all_to_all x1, waiting for transfers between devices, to_all(): lax.all_to_all(jnp.broadcast_to(x[None], (peers,) + x.shape), axes, 0, 0,...  8.41 us
    all_to_all x1, starting transfers between devices, to_all(): lax.all_to_all(jnp.broadcast_to(x[None], (peers,) + x.shape), axes, 0, 0,...  5.85 us
    pallas_call x2, Pallas kernels, sums_of(): call(sums_kernel, (sds((rows, width), F32), sds((rows, width), F32), sds(...  2.61 us
    pallas_call x1, Pallas kernels, grad(): call(functools.partial(grad_kernel, total_rows, steps, along_x), [sds((bl...  2.28 us
  transfers between devices with their start and end apart: 6, of which 5 were waited for; matrix products, arithmetic and copies ran while one was open for 0% of the time, Pallas kernels for 2%

profile of v1, /device:TPU:6, one launch (start us, length us, event | category | flops | bytes accessed | tf_op | source)
XLA Modules:
  0.0 107.7 jit_solution(4628234380947403355)
XLA Ops:
  0.0 0.7 broadcast_in_dim.8
  0.7 25.1 %all_to_all.20 = bf16[4,4,2048]{2,1,0:T(4,128)(2,1)S(1)} all-to-all(bf16[4,4,2048]{2,1,0:T(4,128)(2,1)S(1)} %broadcast_in_dim.8), channel_id=1, replica_groups=mesh['y'=8,'zh'=4,'zl'=3,'x'=4,'c'=2] {'zh'}, dimensions={0} | all-to-all | bytes 131072 | tf_op jit(solution)/shard_map/all_to_all | solution.py:149
  25.8 0.0 copy-start
  25.9 1.0 broadcast_in_dim.10
  26.8 5.8 %all-to-all-start.1 = ((bf16[12,16,2048]{2,1,0:T(8,128)(2,1)}), bf16[12,16,2048]{2,1,0:T(8,128)(2,1)S(1)}, u32[]{:S(2)}, u32[]{:S(2)}) async-start(bf16[12,16,2048]{2,1,0:T(8,128)(2,1)} %broadcast_in_dim.10), calls=%async_computation.1 | async-start | bytes 1572864 | tf_op jit(solution)/shard_map/all_to_all | solution.py:149
  32.7 0.0 copy-done
  32.7 1.9 %collective-permute-start = (bf16[2048,256]{1,0:T(8,128)(2,1)S(1)}, bf16[2048,256]{1,0:T(8,128)(2,1)S(1)}, u32[]{:S(2)}, u32[]{:S(2)}) collective-permute-start(bf16[2048,256]{1,0:T(8,128)(2,1)S(1)} %copy-done), channel_id=1, source_target_pairs={{0,1},{1,0},{2,3},{3,2},{4,5},{5,4},{6,7},{7,6},{8,9},{9,8},{10,11... | collective-permute-start | bytes 3145736 | tf_op jit(solution)/shard_map/ppermute | solution.py:154
  34.6 2.6 %collective-permute-done.dir_ref = bf16[2048,256]{1,0:T(8,128)(2,1)S(1)} collective-permute-done((bf16[2048,256]{1,0:T(8,128)(2,1)S(1)}, bf16[2048,256]{1,0:T(8,128)(2,1)S(1)}, u32[]{:S(2)}, u32[]{:S(2)}) %collective-permute-start) | collective-permute-done | bytes 1048608 | tf_op jit(solution)/shard_map/ppermute | solution.py:154
  37.2 0.3 shard_map.30.unit_ref.more_ref
  37.5 8.4 %all-to-all-done.1 = bf16[12,16,2048]{2,1,0:T(8,128)(2,1)S(1)} async-done(((bf16[12,16,2048]{2,1,0:T(8,128)(2,1)}), bf16[12,16,2048]{2,1,0:T(8,128)(2,1)S(1)}, u32[]{:S(2)}, u32[]{:S(2)}) %all-to-all-start.1) | async-done | bytes 786464 | tf_op jit(solution)/shard_map/all_to_all | solution.py:149
  45.9 1.3 %shard_map.31 = (f32[192,256]{1,0:T(8,128)S(1)}, f32[192,256]{1,0:T(8,128)S(1)}, f32[32,256]{1,0:T(8,128)S(1)}) custom-call(bf16[192,2048]{1,0:T(8,128)(2,1)S(1)} %bitcast.3, bf16[2048,256]{1,0:T(8,128)(2,1)S(1)} %shard_map.30.unit_ref.more_ref), custom_call_target="tpu_custom_call" | custom-call | flops 201326592 | bytes 1572864 | tf_op jit(solution)/shard_map/pallas_call | solution.py:174
  47.2 1.9 %collective-permute-start.1 = (f32[32,256]{1,0:T(8,128)S(1)}, f32[32,256]{1,0:T(8,128)S(1)}, u32[]{:S(2)}, u32[]{:S(2)}) collective-permute-start(f32[32,256]{1,0:T(8,128)S(1)} %get-tuple-element.20), channel_id=1, source_target_pairs={{0,1},{1,0},{2,3},{3,2},{4,5},{5,4},{6,7},{7,6},{8,9},{9,8},{10,11... | collective-permute-start | bytes 98312 | tf_op jit(solution)/shard_map/ppermute | solution.py:154
  49.1 0.3 shard_map.28.unit_ref
  49.4 1.3 %shard_map.29 = (f32[192,256]{1,0:T(8,128)S(1)}, f32[192,256]{1,0:T(8,128)S(1)}, f32[32,256]{1,0:T(8,128)S(1)}) custom-call(bf16[192,2048]{1,0:T(8,128)(2,1)S(1)} %bitcast.4, bf16[2048,256]{1,0:T(8,128)(2,1)S(1)} %shard_map.28.unit_ref), custom_call_target="tpu_custom_call" | custom-call | flops 201326592 | bytes 1572864 | tf_op jit(solution)/shard_map/pallas_call | solution.py:174
  50.7 0.0 collective-permute-done.1
  50.8 18.3 %all_to_all.21 = f16[16,32,256]{2,1,0:T(8,128)(2,1)S(1)} all-to-all(f16[16,32,256]{2,1,0:T(8,128)(2,1)S(1)} %broadcast_in_dim.22), channel_id=1, replica_groups=mesh['y'=8,'zh'=4,'zl'=3,'x'=4,'c'=2] {'y','c'}, dimensions={0} | all-to-all | bytes 524288 | tf_op jit(solution)/shard_map/all_to_all | solution.py:149
  69.1 2.3 %shard_map.32 = (f32[48,2048]{1,0:T(8,128)S(1)}, f32[48,2048]{1,0:T(8,128)S(1)}, f32[48,2048]{1,0:T(8,128)S(1)}, f32[48,2048]{1,0:T(8,128)S(1)}) custom-call(f32[192,256]{1,0:T(8,128)S(1)} %get-tuple-element.15.c_ref, f32[192,256]{1,0:T(8,128)S(1)} %get-tuple-element.16.s_ref, f32[192,256]{1,0:T(8,128)S(1)} %get-tuple-element.17.c2_ref, ...), custom_call_target="tpu_custom_call" | custom-call | flops 402653184 | bytes 1572864 | tf_op jit(solution)/shard_map/pallas_call | solution.py:190
  71.5 1.9 %collective-permute-start.4 = (f16[48,2048]{1,0:T(8,128)(2,1)S(1)}, f16[48,2048]{1,0:T(8,128)(2,1)S(1)}, u32[]{:S(2)}, u32[]{:S(2)}) collective-permute-start(f16[48,2048]{1,0:T(8,128)(2,1)S(1)} %convert_element_type.33), channel_id=1, source_target_pairs={{0,6},{2,0},{4,2},{6,4},{1,7},{3,1},{5,3},{7,5},{8,14},{10,8},{12,... | collective-permute-start | bytes 589832 | tf_op jit(solution)/shard_map/ppermute | solution.py:154
  73.4 5.1 %collective-permute-start.3 = (f16[48,2048]{1,0:T(8,128)(2,1)S(1)}, f16[48,2048]{1,0:T(8,128)(2,1)S(1)}, u32[]{:S(2)}, u32[]{:S(2)}) collective-permute-start(f16[48,2048]{1,0:T(8,128)(2,1)S(1)} %convert_element_type.31), channel_id=1, source_target_pairs={{0,2},{2,4},{4,6},{6,0},{1,3},{3,5},{5,7},{7,1},{8,10},{10,12},{12... | collective-permute-start | bytes 589832 | tf_op jit(solution)/shard_map/ppermute | solution.py:154
  78.5 1.9 %collective-permute-start.2 = (f16[48,2048]{1,0:T(8,128)(2,1)S(1)}, f16[48,2048]{1,0:T(8,128)(2,1)S(1)}, u32[]{:S(2)}, u32[]{:S(2)}) collective-permute-start(f16[48,2048]{1,0:T(8,128)(2,1)S(1)} %convert_element_type.29), channel_id=1, source_target_pairs={{0,4},{2,6},{4,0},{6,2},{1,5},{3,7},{5,1},{7,3},{8,12},{10,14},{12... | collective-permute-start | bytes 589832 | tf_op jit(solution)/shard_map/ppermute | solution.py:154
  80.5 1.8 %collective-permute-done.4 = f16[48,2048]{1,0:T(8,128)(2,1)S(1)} collective-permute-done((f16[48,2048]{1,0:T(8,128)(2,1)S(1)}, f16[48,2048]{1,0:T(8,128)(2,1)S(1)}, u32[]{:S(2)}, u32[]{:S(2)}) %collective-permute-start.4) | collective-permute-done | bytes 196640 | tf_op jit(solution)/shard_map/ppermute | solution.py:154
  82.2 5.4 %collective-permute-done.3 = f16[48,2048]{1,0:T(8,128)(2,1)S(1)} collective-permute-done((f16[48,2048]{1,0:T(8,128)(2,1)S(1)}, f16[48,2048]{1,0:T(8,128)(2,1)S(1)}, u32[]{:S(2)}, u32[]{:S(2)}) %collective-permute-start.3) | collective-permute-done | bytes 196640 | tf_op jit(solution)/shard_map/ppermute | solution.py:154
  87.6 1.4 %collective-permute-done.2 = f16[48,2048]{1,0:T(8,128)(2,1)S(1)} collective-permute-done((f16[48,2048]{1,0:T(8,128)(2,1)S(1)}, f16[48,2048]{1,0:T(8,128)(2,1)S(1)}, u32[]{:S(2)}, u32[]{:S(2)}) %collective-permute-start.2) | collective-permute-done | bytes 196640 | tf_op jit(solution)/shard_map/ppermute | solution.py:154
  89.0 0.1 add_convert_fusion
  89.1 0.1 reshape.17
  89.2 17.8 %all_to_all.22 = f16[12,4,2048]{2,1,0:T(4,128)(2,1)S(1)} all-to-all(f16[12,4,2048]{2,1,0:T(4,128)(2,1)S(1)} %reshape.17), channel_id=1, replica_groups=mesh['y'=8,'zh'=4,'zl'=3,'x'=4,'c'=2] {'zl','zh'}, dimensions={0} | all-to-all | bytes 393216 | tf_op jit(solution)/shard_map/all_to_all | solution.py:204
  107.0 0.7 convert_reduce_fusion
  (7 shorter events, 0.2 us)
Async XLA Ops:
  25.8 6.8 %copy-start = (bf16[2048,256]{1,0:T(8,128)(2,1)S(1)}, bf16[2048,256]{1,0:T(8,128)(2,1)}, u32[]{:S(2)}) copy-start(bf16[2048,256]{1,0:T(8,128)(2,1)} %dir_ref.1) | copy-start | bytes 3145732
  26.8 19.1 %all-to-all-start.1 = ((bf16[12,16,2048]{2,1,0:T(8,128)(2,1)}), bf16[12,16,2048]{2,1,0:T(8,128)(2,1)S(1)}, u32[]{:S(2)}, u32[]{:S(2)}) async-start(bf16[12,16,2048]{2,1,0:T(8,128)(2,1)} %broadcast_in_dim.10), calls=%async_computation.1 | async-start | bytes 1572864 | tf_op jit(solution)/shard_map/all_to_all | solution.py:149
  32.7 4.5 %collective-permute-start = (bf16[2048,256]{1,0:T(8,128)(2,1)S(1)}, bf16[2048,256]{1,0:T(8,128)(2,1)S(1)}, u32[]{:S(2)}, u32[]{:S(2)}) collective-permute-start(bf16[2048,256]{1,0:T(8,128)(2,1)S(1)} %copy-done), channel_id=1, source_target_pairs={{0,1},{1,0},{2,3},{3,2},{4,5},{5,4},{6,7},{7,6},{8,9},{9,8},{10,11... | collective-permute-start | bytes 3145736 | tf_op jit(solution)/shard_map/ppermute | solution.py:154
  47.2 3.5 %collective-permute-start.1 = (f32[32,256]{1,0:T(8,128)S(1)}, f32[32,256]{1,0:T(8,128)S(1)}, u32[]{:S(2)}, u32[]{:S(2)}) collective-permute-start(f32[32,256]{1,0:T(8,128)S(1)} %get-tuple-element.20), channel_id=1, source_target_pairs={{0,1},{1,0},{2,3},{3,2},{4,5},{5,4},{6,7},{7,6},{8,9},{9,8},{10,11... | collective-permute-start | bytes 98312 | tf_op jit(solution)/shard_map/ppermute | solution.py:154
  71.5 10.8 %collective-permute-start.4 = (f16[48,2048]{1,0:T(8,128)(2,1)S(1)}, f16[48,2048]{1,0:T(8,128)(2,1)S(1)}, u32[]{:S(2)}, u32[]{:S(2)}) collective-permute-start(f16[48,2048]{1,0:T(8,128)(2,1)S(1)} %convert_element_type.33), channel_id=1, source_target_pairs={{0,6},{2,0},{4,2},{6,4},{1,7},{3,1},{5,3},{7,5},{8,14},{10,8},{12,... | collective-permute-start | bytes 589832 | tf_op jit(solution)/shard_map/ppermute | solution.py:154
  73.4 14.2 %collective-permute-start.3 = (f16[48,2048]{1,0:T(8,128)(2,1)S(1)}, f16[48,2048]{1,0:T(8,128)(2,1)S(1)}, u32[]{:S(2)}, u32[]{:S(2)}) collective-permute-start(f16[48,2048]{1,0:T(8,128)(2,1)S(1)} %convert_element_type.31), channel_id=1, source_target_pairs={{0,2},{2,4},{4,6},{6,0},{1,3},{3,5},{5,7},{7,1},{8,10},{10,12},{12... | collective-permute-start | bytes 589832 | tf_op jit(solution)/shard_map/ppermute | solution.py:154
  78.5 10.5 %collective-permute-start.2 = (f16[48,2048]{1,0:T(8,128)(2,1)S(1)}, f16[48,2048]{1,0:T(8,128)(2,1)S(1)}, u32[]{:S(2)}, u32[]{:S(2)}) collective-permute-start(f16[48,2048]{1,0:T(8,128)(2,1)S(1)} %convert_element_type.29), channel_id=1, source_target_pairs={{0,4},{2,6},{4,0},{6,2},{1,5},{3,7},{5,1},{7,3},{8,12},{10,14},{12... | collective-permute-start | bytes 589832 | tf_op jit(solution)/shard_map/ppermute | solution.py:154
